TPU v7x, 32 devices: a whole 2x2x4 slice. The times are simulated.
32 devices in a mesh: groups: 2 (over x), tile: 16 (over z, y, core).
Axes of the slice: x: 2, y: 2, z: 4, core: 2. Of those that a mesh axis runs over, the one named last changes fastest.
Arguments:
- grid_tokens: bfloat16 [16384, 512], P(('groups', 'tile')), parts along dimension 0, may hold values from -220 to 220
- obs_features: bfloat16 [65536, 128], P(('groups', 'tile')), parts along dimension 0, may hold values from -45 to 45
- w_obs: bfloat16 [128, 512], replicated, may hold values from -0.5 to 0.5
- b_obs: float32 [512], replicated, may hold values from -4 to 4
- w_query: bfloat16 [512, 512], replicated, may hold values from -0.25 to 0.25
- w_key: bfloat16 [512, 512], replicated, may hold values from -0.25 to 0.25
- w_value: bfloat16 [512, 512], replicated, may hold values from -0.25 to 0.25
- w_out: bfloat16 [512, 512], replicated, may hold values from -0.25 to 0.25
- block_lists: int32 [128, 32], P('groups'), parts along dimension 0, may hold values from 0 to 511, as said below
- block_counts: int32 [128], P('groups'), parts along dimension 0, may hold values from 24 to 32, as said below
- block_position: int32 [1024], P('groups'), parts along dimension 0, may hold values from 0 to 511, as said below
- proc_order: int32 [128], P('groups'), parts along dimension 0, may hold values from 0 to 63, each once
Outputs:
- arranged: bfloat16 [16384, 512], P(('groups', 'tile')), parts along dimension 0
There are 2 independent parts, one for each index of `groups`. A program takes and returns all parts, laid end to end along the dimension named above; an argument that names none is the same for every part. Nothing has to cross between parts.
Inputs may be any that keep to these rules, and one draw needn't show every extreme that they name: `block_lists`: over the entries below block_counts of the 4 tiles t of one device (t // 4 equal), at most 16 name blocks whose storage position // 32 is any one device; in every draw some device has exactly 16 from some device. `block_counts`: some tile uses all 32 entries. `block_position`: A permutation of the storage positions.
All inputs are finite; a program needn't handle non-finite values.
Results may differ from a plain program's by a relative error of at most 0.012.
The roundings to bfloat16 on the way count: a program that leaves them out, or rounds other values in their place, can miss the bound.
Values may be sent and summed in bfloat16 or wider, within the bound.
A program may use at most 128 MiB of HBM per device.

v0:
```python
import jax
import jax.numpy as jnp
from jax import lax
from jax.sharding import PartitionSpec as P

HEADS = 8
BLOCK = 64
NSEL = 32
TILE_ROWS = 128


def embed_rows(feats, feat_mean, feat_rstd, w_obs, b_obs):
    normed = ((feats.astype(jnp.float32) - feat_mean) * feat_rstd).astype(jnp.bfloat16)
    hidden = jnp.dot(normed, w_obs, preferred_element_type=jnp.float32) + b_obs
    return jax.nn.gelu(hidden, approximate=True).astype(jnp.bfloat16)


def local(
    grid_tokens,
    obs_features,
    w_obs,
    b_obs,
    w_query,
    w_key,
    w_value,
    w_out,
    block_lists,
    block_counts,
    block_position,
    proc_order,
):
    tile_count = lax.axis_size("tile")
    own_index = lax.axis_index("tile")
    obs_blocks = obs_features.shape[0] // BLOCK
    tile_local = grid_tokens.shape[0] // TILE_ROWS
    entry_count = tile_local * NSEL
    capacity = max(2, 2 * entry_count // tile_count)
    width = grid_tokens.shape[1]
    obs_wide = obs_features.astype(jnp.float32)
    first_sum, second_sum = lax.psum(
        (jnp.sum(obs_wide, axis=0), jnp.sum(obs_wide * obs_wide, axis=0)), "tile"
    )
    obs_total = obs_features.shape[0] * tile_count
    feat_mean = first_sum / obs_total
    feat_rstd = lax.rsqrt(second_sum / obs_total - feat_mean * feat_mean + 1e-05)
    spots = jnp.take(block_position, block_lists, axis=0)
    is_valid = jnp.arange(NSEL, dtype=jnp.int32)[None, :] < block_counts[:, None]
    owner_dev = (spots // obs_blocks).reshape(tile_count, entry_count)
    local_blk = (spots % obs_blocks).reshape(tile_count, entry_count)
    valid_rows = is_valid.reshape(tile_count, entry_count)
    entry_order = jnp.arange(entry_count, dtype=jnp.int32)
    earlier = (
        (owner_dev[:, :, None] == owner_dev[:, None, :])
        & valid_rows[:, None, :]
        & (entry_order[None, :] < entry_order[:, None])[None, :, :]
    )
    slot_rank = jnp.sum(earlier.astype(jnp.int32), axis=2)
    mine = valid_rows & (owner_dev == own_index)
    slot_ids = jnp.arange(capacity, dtype=jnp.int32)
    hits = mine[:, None, :] & (slot_rank[:, None, :] == slot_ids[None, :, None])
    present = jnp.any(hits, axis=2)
    slot_block = jnp.sum(jnp.where(hits, local_blk[:, None, :], 0), axis=2)
    my_owner = lax.dynamic_index_in_dim(owner_dev, own_index, 0, keepdims=False)
    my_rank = lax.dynamic_index_in_dim(slot_rank, own_index, 0, keepdims=False)
    my_valid = lax.dynamic_index_in_dim(valid_rows, own_index, 0, keepdims=False)
    pick_slot = jnp.where(my_valid, my_owner * capacity + my_rank, 0)
    raw_blocks = obs_features.reshape(obs_blocks, BLOCK, obs_features.shape[1])
    chosen = jnp.take(raw_blocks, slot_block, axis=0)
    incoming = lax.all_to_all(
        jnp.where(present[:, :, None, None], chosen, jnp.zeros((), raw_blocks.dtype)),
        "tile",
        split_axis=0,
        concat_axis=0,
        tiled=True,
    )
    flat_blocks = incoming.reshape(tile_count * capacity, BLOCK, incoming.shape[3])
    chosen_rows = embed_rows(
        jnp.take(flat_blocks, pick_slot, axis=0).reshape(entry_count * BLOCK, incoming.shape[3]),
        feat_mean,
        feat_rstd,
        w_obs,
        b_obs,
    )
    key_rows = jnp.dot(chosen_rows, w_key, preferred_element_type=jnp.float32).astype(jnp.bfloat16)
    value_rows = jnp.dot(chosen_rows, w_value, preferred_element_type=jnp.float32).astype(
        jnp.bfloat16
    )
    query_rows = jnp.dot(grid_tokens, w_query, preferred_element_type=jnp.float32).astype(
        jnp.bfloat16
    )
    my_counts = lax.dynamic_slice_in_dim(block_counts, own_index * tile_local, tile_local)
    head_dim = width // HEADS
    scale = 1.0 / head_dim**0.5
    key_span = NSEL * BLOCK
    results = []
    for tile_pos in range(tile_local):
        query_tile = query_rows[tile_pos * TILE_ROWS : (tile_pos + 1) * TILE_ROWS]
        key_tile = key_rows[tile_pos * key_span : (tile_pos + 1) * key_span]
        value_tile = value_rows[tile_pos * key_span : (tile_pos + 1) * key_span]
        keymask = jnp.repeat(jnp.arange(NSEL, dtype=jnp.int32) < my_counts[tile_pos], BLOCK)

        def one_head(
            head, query_tile=query_tile, key_tile=key_tile, value_tile=value_tile, keymask=keymask
        ):
            query_head = lax.dynamic_slice_in_dim(query_tile, head * head_dim, head_dim, 1)
            key_head = lax.dynamic_slice_in_dim(key_tile, head * head_dim, head_dim, 1)
            value_head = lax.dynamic_slice_in_dim(value_tile, head * head_dim, head_dim, 1)
            scores = (
                lax.dot_general(
                    query_head,
                    key_head,
                    (((1,), (1,)), ((), ())),
                    preferred_element_type=jnp.float32,
                )
                * scale
            )
            scores = jnp.where(keymask[None, :], scores, jnp.float32(-1e30))
            peak = jnp.max(scores, axis=-1, keepdims=True)
            expo = jnp.exp(scores - peak)
            totals = jnp.sum(expo, axis=-1, keepdims=True)
            weights_bf = expo.astype(jnp.bfloat16)
            return jnp.dot(weights_bf, value_head, preferred_element_type=jnp.float32) / totals

        per_head = lax.map(one_head, jnp.arange(HEADS, dtype=jnp.int32))
        results.append(
            jnp.transpose(per_head, (1, 0, 2)).reshape(TILE_ROWS, width).astype(jnp.bfloat16)
        )
    attended = jnp.concatenate(results, axis=0)
    encoded = jnp.dot(attended, w_out, preferred_element_type=jnp.float32).astype(jnp.bfloat16)
    outgoing = encoded.reshape(tile_local, tile_count, TILE_ROWS // tile_count, width)
    arrived = lax.all_to_all(outgoing, "tile", split_axis=1, concat_axis=0, tiled=True)
    arrived = arrived.reshape(tile_count * tile_local, TILE_ROWS // tile_count, width)
    return jnp.take(arrived, proc_order, axis=0).reshape(
        tile_count * tile_local * (TILE_ROWS // tile_count), width
    )


def solution(mesh):
    in_specs = (
        P(("groups", "tile"), None),
        P(("groups", "tile"), None),
        P(),
        P(),
        P(),
        P(),
        P(),
        P(),
        P("groups", None),
        P("groups"),
        P("groups"),
        P("groups"),
    )
    out_specs = P(("groups", "tile"), None)
    return jax.shard_map(local, mesh=mesh, in_specs=in_specs, out_specs=out_specs, check_vma=False)
```

profile of v0, /device:TPU:0, one launch (start us, length us, event | category | flops | bytes accessed | tf_op | source)
XLA Modules:
  0.0 354.2 jit_solution(3823423452104202265)
XLA Ops:
  1.0 13.2 %gather_fusion = s32[2048]{0:T(1024)S(1)} fusion(s32[512]{0:T(512)S(1)} %copy-done.2, s32[2048]{0:T(1024)S(1)} %broadcast_clamp_fusion), kind=kCustom, calls=%fused_computation | custom fusion | bytes 24576 | tf_op jit(solution)/shard_map/jit(_take)/gather | solution.py:46
  16.2 3.1 gather_fusion.1
  19.3 3.9 %select_select_fusion = bf16[16,16,64,128]{3,2,1,0:T(8,128)(2,1)} fusion(bf16[16,16,64,128]{3,2,1,0:T(8,128)(2,1)} %bitcast.84, pred[16,16]{1,0:T(8,128)(4,1)S(1)} %compare_and_fusion, pred[16,16]{1,0:T(8,128)(4,1)S(1)} %fusion.75), kind=kLoop, calls=%fused_computation.76 | loop fusion | flops 4194304 | bytes 8389120 | tf_op jit(solution)/shard_map/jit(_where)/select_n | solution.py:70
  23.2 7.6 %all-to-all-start = ((bf16[16,16,64,128]{3,2,1,0:T(8,128)(2,1)}), bf16[16,16,64,128]{3,2,1,0:T(8,128)(2,1)}, u32[]{:S(2)}, u32[]{:S(2)}) async-start(bf16[16,16,64,128]{3,2,1,0:T(8,128)(2,1)} %select_select_fusion), calls=%async_computation | async-start | bytes 8388608 | tf_op jit(solution)/shard_map/all_to_all | solution.py:69
  31.4 95.8 %all-reduce = (f32[128]{0:T(128)S(1)}, f32[128]{0:T(128)S(1)}) all-reduce(f32[128]{0:T(128)S(1)} %get-tuple-element.226, f32[128]{0:T(128)S(1)} %get-tuple-element.225), channel_id=1, replica_groups=mesh['groups'=2,'tile'=16] {'tile'}, use_global_device_ids=true, to_apply=%region_6.7 | all-reduce | flops 256 | bytes 2048 | tf_op jit(solution)/shard_map/psum | solution.py:40
  130.8 3.2 gather_fusion.2
  134.0 4.3 %bitcast_select_fusion = bf16[8192,128]{1,0:T(8,128)(2,1)S(1)} fusion(bf16[128,64,128]{2,1,0:T(8,128)(2,1)S(1)} %gather_fusion.2, pred[8192]{0:T(1024)(128)(4,1)S(1)} %broadcast_in_dim.178), kind=kLoop, calls=%fused_computation.77 | loop fusion | flops 1048576 | bytes 4202496 | tf_op jit(solution)/shard_map/jit(_take)/select_n | solution.py:78
  138.3 6.6 %fusion.63 = bf16[8192,512]{1,0:T(8,128)(2,1)S(1)} fusion(bf16[128,512]{1,0:T(8,128)(2,1)S(1)} %copy-done.8, f32[512]{0:T(512)S(1)} %copy-done.9, bf16[8192,128]{1,0:T(8,128)(2,1)S(1)} %bitcast_select_fusion, f32[128]{0:T(128)S(1)} %get-tuple-element.315, f32[128]{0:T(128)S(1)} %get-tuple-element.314), kind=kOutput, calls=%fused_computation.72 | convolution fusion | flops 1119879168 | bytes 10619904 | tf_op jit(solution)/shard_map/dot_general | solution.py:14
  144.9 3.2 copy-done.11
  148.1 4.7 %convolution_convert_fusion = bf16[8192,512]{1,0:T(8,128)(2,1)S(1)} fusion(bf16[8192,512]{1,0:T(8,128)(2,1)S(1)} %fusion.63, bf16[512,512]{1,0:T(8,128)(2,1)S(1)} %copy-done), kind=kOutput, calls=%fused_computation.73 | convolution fusion | flops 4299161600 | bytes 17301504 | tf_op jit(solution)/shard_map/dot_general | solution.py:85
  152.9 8.1 %convolution_convert_fusion.1 = bf16[8192,512]{1,0:T(8,128)(2,1)S(1)} fusion(bf16[8192,512]{1,0:T(8,128)(2,1)} %copy-done.11, bf16[512,512]{1,0:T(8,128)(2,1)S(1)} %copy-done.7), kind=kOutput, calls=%fused_computation.74 | convolution fusion | flops 4299161600 | bytes 17301504 | tf_op jit(solution)/shard_map/dot_general | solution.py:84
  161.0 5.2 %fusion.86 = (bf16[2048,512]{1,0:T(8,128)(2,1)}, bf16[2048,512]{1,0:T(8,128)(2,1)S(1)}, bf16[2048,512]{1,0:T(8,128)(2,1)}, bf16[2048,512]{1,0:T(8,128)(2,1)}, bf...) fusion(bf16[8192,512]{1,0:T(8,128)(2,1)S(1)} %convolution_conver, ...), kind=kLoop, calls=%fused_computation.140 | loop fusion | bytes 33554432 | tf_op jit(solution)/shard_map/slice | solution.py:99
  166.2 40.6 %while.44 = (s32[]{:T(128)}, bf16[8,128,64]{1,2,0:T(8,128)(2,1)S(1)}, s32[8]{0:T(128)S(1)}, bf16[128,512]{1,0:T(8,128)(2,1)S(1)}, bf16[2048,512]{1,0:T(8,128)(2,...) while((s32[]{:T(128)}, ...), condition=%wide.region_10.11_spmd.clone, body=%wide.region_7.10_spmd.clone.sunk | while | flops 68951808 | bytes 4272331 | solution.py:124
  169.6 1.7 fusion.122
  174.7 1.7 fusion.122
  179.7 1.7 fusion.122
  184.8 1.7 fusion.122
  189.9 1.7 fusion.122
  194.9 1.7 fusion.122
  200.0 1.7 fusion.122
  205.1 1.7 fusion.122
  206.8 40.2 %while.45 = (s32[]{:T(128)}, bf16[8,128,64]{1,2,0:T(8,128)(2,1)S(1)}, s32[8]{0:T(128)S(1)}, bf16[128,512]{1,0:T(8,128)(2,1)S(1)}, bf16[2048,512]{1,0:T(8,128)(2,...) while((s32[]{:T(128)}, ...), condition=%wide.region_14.15_spmd.clone, body=%wide.region_11.14_spmd.clone.sunk | while | flops 68951808 | bytes 4272331 | solution.py:124
  208.3 1.5 fusion.125
  210.1 1.7 fusion.127
  215.2 1.7 fusion.127
  220.2 1.7 fusion.127
  225.2 1.7 fusion.127
  230.3 1.7 fusion.127
  235.3 1.7 fusion.127
  240.3 1.7 fusion.127
  245.3 1.7 fusion.127
  247.1 39.2 %while.46 = (s32[]{:T(128)}, bf16[8,128,64]{1,2,0:T(8,128)(2,1)S(1)}, s32[8]{0:T(128)S(1)}, bf16[128,512]{1,0:T(8,128)(2,1)S(1)}, bf16[2048,512]{1,0:T(8,128)(2,...) while((s32[]{:T(128)}, ...), condition=%wide.region_18.19_spmd.clone, body=%wide.region_15.18_spmd.clone.sunk | while | flops 68951808 | bytes 4272331 | solution.py:124
  248.7 1.5 fusion.130
  250.5 1.7 fusion.132
  255.4 1.7 fusion.132
  260.2 1.7 fusion.132
  265.1 1.7 fusion.132
  270.0 1.7 fusion.132
  274.9 1.7 fusion.132
  279.7 1.7 fusion.132
  284.6 1.7 fusion.132
  286.4 31.1 %while.47 = (s32[]{:T(128)}, bf16[8,128,64]{1,2,0:T(8,128)(2,1)S(1)}, s32[8]{0:T(128)S(1)}, bf16[128,512]{1,0:T(8,128)(2,1)S(1)}, bf16[2048,512]{1,0:T(8,128)(2,...) while((s32[]{:T(128)}, ...), condition=%wide.region_22.23_spmd.clone, body=%wide.region_19.22_spmd.clone.sunk | while | flops 68951808 | bytes 4271823 | solution.py:124
  287.8 1.5 fusion.135
  307.2 1.5 fusion.135
  311.1 1.5 fusion.135
  317.5 1.6 convolution_convert_fusion.2
  319.9 18.5 %all-to-all-start.1 = ((bf16[4,16,8,512]{3,2,0,1:T(8,128)(2,1)}), bf16[4,16,8,512]{3,2,0,1:T(8,128)(2,1)S(1)}, u32[]{:S(2)}, u32[]{:S(2)}) async-start(bf16[4,16,8,512]{3,2,0,1:T(8,128)(2,1)} %copy.20), calls=%async_computation.1 | async-start | bytes 1048576 | tf_op jit(solution)/shard_map/all_to_all | solution.py:131
  338.6 14.0 %all-to-all-done.1 = bf16[4,16,8,512]{3,2,0,1:T(8,128)(2,1)S(1)} async-done(((bf16[4,16,8,512]{3,2,0,1:T(8,128)(2,1)}), bf16[4,16,8,512]{3,2,0,1:T(8,128)(2,1)S(1)}, u32[]{:S(2)}, u32[]{:S(2)}) %all-to-all-start.1) | async-done | bytes 524320 | tf_op jit(solution)/shard_map/all_to_all | solution.py:131
  (240 shorter events, 90.6 us)
Async XLA Ops:
  0.0 148.1 %copy-start = (bf16[512,512]{1,0:T(8,128)(2,1)S(1)}, bf16[512,512]{1,0:T(8,128)(2,1)}, u32[]{:S(2)}) copy-start(bf16[512,512]{1,0:T(8,128)(2,1)} %param.26) | copy-start | bytes 1572868
  0.0 1.0 copy-start.2
  1.0 13.4 %copy-start.6 = (s32[64]{0:T(128)S(1)}, s32[64]{0:T(128)}, u32[]{:S(2)}) copy-start(s32[64]{0:T(128)} %param.29) | copy-start | bytes 772
  1.0 15.2 %copy-start.3 = (bf16[2048,128]{1,0:T(8,128)(2,1)S(1)}, bf16[2048,128]{1,0:T(8,128)(2,1)}, u32[]{:S(2)}) copy-start(bf16[2048,128]{1,0:T(8,128)(2,1)} %param.21) | copy-start | bytes 1572868
  23.2 107.1 %copy-start.4 = (bf16[512,512]{1,0:T(8,128)(2,1)S(1)}, bf16[512,512]{1,0:T(8,128)(2,1)}, u32[]{:S(2)}) copy-start(bf16[512,512]{1,0:T(8,128)(2,1)} %param.20) | copy-start | bytes 1572868
  23.2 107.1 %copy-start.5 = (bf16[512,512]{1,0:T(8,128)(2,1)S(1)}, bf16[512,512]{1,0:T(8,128)(2,1)}, u32[]{:S(2)}) copy-start(bf16[512,512]{1,0:T(8,128)(2,1)} %param.24) | copy-start | bytes 1572868
  23.2 107.6 %all-to-all-start = ((bf16[16,16,64,128]{3,2,1,0:T(8,128)(2,1)}), bf16[16,16,64,128]{3,2,1,0:T(8,128)(2,1)}, u32[]{:S(2)}, u32[]{:S(2)}) async-start(bf16[16,16,64,128]{3,2,1,0:T(8,128)(2,1)} %select_select_fusion), calls=%async_computation | async-start | bytes 8388608 | tf_op jit(solution)/shard_map/all_to_all | solution.py:69
  130.8 7.5 %copy-start.8 = (bf16[128,512]{1,0:T(8,128)(2,1)S(1)}, bf16[128,512]{1,0:T(8,128)(2,1)}, u32[]{:S(2)}) copy-start(bf16[128,512]{1,0:T(8,128)(2,1)} %param.22) | copy-start | bytes 393220
  130.8 7.5 %copy-start.9 = (f32[512]{0:T(512)S(1)}, f32[512]{0:T(512)}, u32[]{:S(2)}) copy-start(f32[512]{0:T(512)} %param.23) | copy-start | bytes 6148
  144.9 3.2 copy-start.11
  148.1 4.7 %copy-start.7 = (bf16[512,512]{1,0:T(8,128)(2,1)S(1)}, bf16[512,512]{1,0:T(8,128)(2,1)}, u32[]{:S(2)}) copy-start(bf16[512,512]{1,0:T(8,128)(2,1)} %param.25) | copy-start | bytes 1572868
  317.5 21.0 %copy-start.10 = (s32[64]{0:T(128)S(1)}, s32[64]{0:T(128)}, u32[]{:S(2)}) copy-start(s32[64]{0:T(128)} %param.31) | copy-start | bytes 772
  317.5 36.7 %copy-start.1 = (bf16[512,512]{1,0:T(8,128)(2,1)S(1)}, bf16[512,512]{1,0:T(8,128)(2,1)}, u32[]{:S(2)}) copy-start(bf16[512,512]{1,0:T(8,128)(2,1)} %param.26) | copy-start | bytes 1572868
  319.9 32.8 %all-to-all-start.1 = ((bf16[4,16,8,512]{3,2,0,1:T(8,128)(2,1)}), bf16[4,16,8,512]{3,2,0,1:T(8,128)(2,1)S(1)}, u32[]{:S(2)}, u32[]{:S(2)}) async-start(bf16[4,16,8,512]{3,2,0,1:T(8,128)(2,1)} %copy.20), calls=%async_computation.1 | async-start | bytes 1048576 | tf_op jit(solution)/shard_map/all_to_all | solution.py:131
where the time goes:
time: 358 us; the launch traced here: 354 us
  matrix products  116 us (32%)
  blocking collectives  95.8 us (27%)
  local copies, waits for them, and re-layouts  57.2 us (16%)
  starting transfers between devices  26.1 us (7%)
  other arithmetic  23 us (6%)
  loops' own time  21.6 us (6%)
  waiting for transfers between devices  14 us (4%)
    psum x1, blocking collectives, local(): lax.psum((jnp.sum(obs_wide, axis=0), jnp.sum(obs_wide * obs_wide, axis=0)...  95.8 us
    dot_general x32, matrix products, one_head(): lax.dot_general(query_head, key_head, (((1,), (1,)), ((), ())), preferred...  48.2 us
    dot_general x32, matrix products, one_head(): jnp.dot(weights_bf, value_head, preferred_element_type=jnp.float32) / totals  46.3 us
    another operation x4, loops' own time, local(): per_head = lax.map(one_head, jnp.arange(HEADS, dtype=jnp.int32))  21.6 us
    dynamic_slice x32, local copies, waits for them, and re-layouts, local(): per_head = lax.map(one_head, jnp.arange(HEADS, dtype=jnp.int32))  20 us
    all_to_all x1, starting transfers between devices, local(): lax.all_to_all(outgoing, 'tile', split_axis=1, concat_axis=0, tiled=True)  18.5 us
    all_to_all x1, waiting for transfers between devices, local(): lax.all_to_all(outgoing, 'tile', split_axis=1, concat_axis=0, tiled=True)  14 us
    gather x2, local copies, waits for them, and re-layouts, local(): spots = jnp.take(block_position, block_lists, axis=0)  13.3 us
  transfers between devices with their start and end apart: 2, of which 1 were waited for; matrix products, arithmetic and copies ran while one was open for 1% of the time, Pallas kernels for 0%

commit v1 on v0

--- a/solution.py
+++ b/solution.py
@@ -128,7 +128,10 @@
     attended = jnp.concatenate(results, axis=0)
     encoded = jnp.dot(attended, w_out, preferred_element_type=jnp.float32).astype(jnp.bfloat16)
     outgoing = encoded.reshape(tile_local, tile_count, TILE_ROWS // tile_count, width)
-    arrived = lax.all_to_all(outgoing, "tile", split_axis=1, concat_axis=0, tiled=True)
+    arrived = jnp.concatenate(
+        lax.all_to_all(jnp.stack(jnp.split(outgoing, lax.axis_size("tile"), axis=1)), "tile", 0, 0),
+        axis=0,
+    )
     arrived = arrived.reshape(tile_count * tile_local, TILE_ROWS // tile_count, width)
     return jnp.take(arrived, proc_order, axis=0).reshape(
         tile_count * tile_local * (TILE_ROWS // tile_count), width

time: 358 us -> 367 us (1.025)
  local copies, waits for them, and re-layouts: 57.2 us -> 66.2 us
    unnamed x25 -> x40, local copies, waits for them, and re-layouts: 4.12 us -> 13.4 us
where the time goes in v1:
time: 367 us; the launch traced here: 363 us
  matrix products  116 us (32%)
  blocking collectives  95.8 us (26%)
  local copies, waits for them, and re-layouts  66.2 us (18%)
  starting transfers between devices  26.1 us (7%)
  other arithmetic  23 us (6%)
  loops' own time  21.6 us (6%)
  waiting for transfers between devices  14 us (4%)
    psum x1, blocking collectives, local(): lax.psum((jnp.sum(obs_wide, axis=0), jnp.sum(obs_wide * obs_wide, axis=0)...  95.8 us
    dot_general x32, matrix products, one_head(): lax.dot_general(query_head, key_head, (((1,), (1,)), ((), ())), preferred...  48.2 us
    dot_general x32, matrix products, one_head(): jnp.dot(weights_bf, value_head, preferred_element_type=jnp.float32) / totals  46.3 us
    another operation x4, loops' own time, local(): per_head = lax.map(one_head, jnp.arange(HEADS, dtype=jnp.int32))  21.6 us
    dynamic_slice x32, local copies, waits for them, and re-layouts, local(): per_head = lax.map(one_head, jnp.arange(HEADS, dtype=jnp.int32))  20 us
    all_to_all x1, starting transfers between devices, local(): lax.all_to_all(jnp.stack(jnp.split(outgoing, lax.axis_size('tile'), axis=...  18.5 us
    all_to_all x1, waiting for transfers between devices, local(): lax.all_to_all(jnp.stack(jnp.split(outgoing, lax.axis_size('tile'), axis=...  14 us
    unnamed x40, local copies, waits for them, and re-layouts  13.4 us
  transfers between devices with their start and end apart: 2, of which 1 were waited for; matrix products, arithmetic and copies ran while one was open for 1% of the time, Pallas kernels for 0%

profile of v1, /device:TPU:0, one launch (start us, length us, event | category | flops | bytes accessed | tf_op | source)
XLA Modules:
  0.0 363.3 jit_solution(9890412594102539912)
XLA Ops:
  1.0 13.2 %gather_fusion = s32[2048]{0:T(1024)S(1)} fusion(s32[512]{0:T(512)S(1)} %copy-done.2, s32[2048]{0:T(1024)S(1)} %broadcast_clamp_fusion), kind=kCustom, calls=%fused_computation | custom fusion | bytes 24576 | tf_op jit(solution)/shard_map/jit(_take)/gather | solution.py:46
  16.2 3.1 gather_fusion.1
  19.3 3.9 %select_select_fusion = bf16[16,16,64,128]{3,2,1,0:T(8,128)(2,1)} fusion(bf16[16,16,64,128]{3,2,1,0:T(8,128)(2,1)} %bitcast.174, pred[16,16]{1,0:T(8,128)(4,1)S(1)} %compare_and_fusion, pred[16,16]{1,0:T(8,128)(4,1)S(1)} %fusion.75), kind=kLoop, calls=%fused_computation.76 | loop fusion | flops 4194304 | bytes 8389120 | tf_op jit(solution)/shard_map/jit(_where)/select_n | solution.py:70
  23.2 7.6 %all-to-all-start = ((bf16[16,16,64,128]{3,2,1,0:T(8,128)(2,1)}), bf16[16,16,64,128]{3,2,1,0:T(8,128)(2,1)}, u32[]{:S(2)}, u32[]{:S(2)}) async-start(bf16[16,16,64,128]{3,2,1,0:T(8,128)(2,1)} %select_select_fusion), calls=%async_computation | async-start | bytes 8388608 | tf_op jit(solution)/shard_map/all_to_all | solution.py:69
  31.4 95.8 %all-reduce = (f32[128]{0:T(128)S(1)}, f32[128]{0:T(128)S(1)}) all-reduce(f32[128]{0:T(128)S(1)} %get-tuple-element.226, f32[128]{0:T(128)S(1)} %get-tuple-element.225), channel_id=1, replica_groups=mesh['groups'=2,'tile'=16] {'tile'}, use_global_device_ids=true, to_apply=%region_6.7 | all-reduce | flops 256 | bytes 2048 | tf_op jit(solution)/shard_map/psum | solution.py:40
  130.8 3.2 gather_fusion.2
  134.0 4.3 %bitcast_select_fusion = bf16[8192,128]{1,0:T(8,128)(2,1)S(1)} fusion(bf16[128,64,128]{2,1,0:T(8,128)(2,1)S(1)} %gather_fusion.2, pred[8192]{0:T(1024)(128)(4,1)S(1)} %broadcast_in_dim.178), kind=kLoop, calls=%fused_computation.77 | loop fusion | flops 1048576 | bytes 4202496 | tf_op jit(solution)/shard_map/jit(_take)/select_n | solution.py:78
  138.3 6.6 %fusion.63 = bf16[8192,512]{1,0:T(8,128)(2,1)S(1)} fusion(bf16[128,512]{1,0:T(8,128)(2,1)S(1)} %copy-done.8, f32[512]{0:T(512)S(1)} %copy-done.9, bf16[8192,128]{1,0:T(8,128)(2,1)S(1)} %bitcast_select_fusion, f32[128]{0:T(128)S(1)} %get-tuple-element.315, f32[128]{0:T(128)S(1)} %get-tuple-element.314), kind=kOutput, calls=%fused_computation.72 | convolution fusion | flops 1119879168 | bytes 10619904 | tf_op jit(solution)/shard_map/dot_general | solution.py:14
  144.9 3.2 copy-done.11
  148.1 4.7 %convolution_convert_fusion = bf16[8192,512]{1,0:T(8,128)(2,1)S(1)} fusion(bf16[8192,512]{1,0:T(8,128)(2,1)S(1)} %fusion.63, bf16[512,512]{1,0:T(8,128)(2,1)S(1)} %copy-done), kind=kOutput, calls=%fused_computation.73 | convolution fusion | flops 4299161600 | bytes 17301504 | tf_op jit(solution)/shard_map/dot_general | solution.py:85
  152.9 8.1 %convolution_convert_fusion.1 = bf16[8192,512]{1,0:T(8,128)(2,1)S(1)} fusion(bf16[8192,512]{1,0:T(8,128)(2,1)} %copy-done.11, bf16[512,512]{1,0:T(8,128)(2,1)S(1)} %copy-done.7), kind=kOutput, calls=%fused_computation.74 | convolution fusion | flops 4299161600 | bytes 17301504 | tf_op jit(solution)/shard_map/dot_general | solution.py:84
  161.0 5.2 %fusion.102 = (bf16[2048,512]{1,0:T(8,128)(2,1)}, bf16[2048,512]{1,0:T(8,128)(2,1)S(1)}, bf16[2048,512]{1,0:T(8,128)(2,1)}, bf16[2048,512]{1,0:T(8,128)(2,1)}, b...) fusion(bf16[8192,512]{1,0:T(8,128)(2,1)S(1)} %convolution_conve, ...), kind=kLoop, calls=%fused_computation.172 | loop fusion | bytes 33554432 | tf_op jit(solution)/shard_map/slice | solution.py:99
  166.2 40.6 %while.44 = (s32[]{:T(128)}, bf16[8,128,64]{1,2,0:T(8,128)(2,1)S(1)}, s32[8]{0:T(128)S(1)}, bf16[128,512]{1,0:T(8,128)(2,1)S(1)}, bf16[2048,512]{1,0:T(8,128)(2,...) while((s32[]{:T(128)}, ...), condition=%wide.region_10.11_spmd.clone, body=%wide.region_7.10_spmd.clone.sunk | while | flops 68951808 | bytes 4272331 | solution.py:124
  169.6 1.7 fusion.138
  174.7 1.7 fusion.138
  179.7 1.7 fusion.138
  184.8 1.7 fusion.138
  189.9 1.7 fusion.138
  194.9 1.7 fusion.138
  200.0 1.7 fusion.138
  205.1 1.7 fusion.138
  206.8 40.2 %while.45 = (s32[]{:T(128)}, bf16[8,128,64]{1,2,0:T(8,128)(2,1)S(1)}, s32[8]{0:T(128)S(1)}, bf16[128,512]{1,0:T(8,128)(2,1)S(1)}, bf16[2048,512]{1,0:T(8,128)(2,...) while((s32[]{:T(128)}, ...), condition=%wide.region_14.15_spmd.clone, body=%wide.region_11.14_spmd.clone.sunk | while | flops 68951808 | bytes 4272331 | solution.py:124
  208.3 1.5 fusion.141
  210.1 1.7 fusion.143
  215.2 1.7 fusion.143
  220.2 1.7 fusion.143
  225.2 1.7 fusion.143
  230.3 1.7 fusion.143
  235.3 1.7 fusion.143
  240.3 1.7 fusion.143
  245.3 1.7 fusion.143
  247.1 39.2 %while.46 = (s32[]{:T(128)}, bf16[8,128,64]{1,2,0:T(8,128)(2,1)S(1)}, s32[8]{0:T(128)S(1)}, bf16[128,512]{1,0:T(8,128)(2,1)S(1)}, bf16[2048,512]{1,0:T(8,128)(2,...) while((s32[]{:T(128)}, ...), condition=%wide.region_18.19_spmd.clone, body=%wide.region_15.18_spmd.clone.sunk | while | flops 68951808 | bytes 4272331 | solution.py:124
  248.7 1.5 fusion.146
  250.5 1.7 fusion.148
  255.4 1.7 fusion.148
  260.2 1.7 fusion.148
  265.1 1.7 fusion.148
  270.0 1.7 fusion.148
  274.9 1.7 fusion.148
  279.7 1.7 fusion.148
  284.6 1.7 fusion.148
  286.4 31.1 %while.47 = (s32[]{:T(128)}, bf16[8,128,64]{1,2,0:T(8,128)(2,1)S(1)}, s32[8]{0:T(128)S(1)}, bf16[128,512]{1,0:T(8,128)(2,1)S(1)}, bf16[2048,512]{1,0:T(8,128)(2,...) while((s32[]{:T(128)}, ...), condition=%wide.region_22.23_spmd.clone, body=%wide.region_19.22_spmd.clone.sunk | while | flops 68951808 | bytes 4271823 | solution.py:124
  287.8 1.5 fusion.151
  307.2 1.5 fusion.151
  311.1 1.5 fusion.151
  317.5 1.6 convolution_convert_fusion.2
  328.9 18.5 %all-to-all-start.1 = ((bf16[16,4,1,8,512]{4,3,1,2,0:T(8,128)(2,1)}), bf16[16,4,1,8,512]{4,3,1,2,0:T(8,128)(2,1)S(1)}, u32[]{:S(2)}, u32[]{:S(2)}) async-start(bf16[16,4,1,8,512]{4,3,1,2,0:T(8,128)(2,1)} %fusion.76), calls=%async_computation.1 | async-start | bytes 1048576 | tf_op jit(solution)/shard_map/all_to_all | solution.py:132
  347.7 14.0 %all-to-all-done.1 = bf16[16,4,1,8,512]{4,3,1,2,0:T(8,128)(2,1)S(1)} async-done(((bf16[16,4,1,8,512]{4,3,1,2,0:T(8,128)(2,1)}), bf16[16,4,1,8,512]{4,3,1,2,0:T(8,128)(2,1)S(1)}, u32[]{:S(2)}, u32[]{:S(2)}) %all-to-all-start.1) | async-done | bytes 524320 | tf_op jit(solution)/shard_map/all_to_all | solution.py:132
  (255 shorter events, 99.7 us)
Async XLA Ops:
  0.0 148.1 %copy-start = (bf16[512,512]{1,0:T(8,128)(2,1)S(1)}, bf16[512,512]{1,0:T(8,128)(2,1)}, u32[]{:S(2)}) copy-start(bf16[512,512]{1,0:T(8,128)(2,1)} %param.26) | copy-start | bytes 1572868
  0.0 1.0 copy-start.2
  1.0 13.4 %copy-start.6 = (s32[64]{0:T(128)S(1)}, s32[64]{0:T(128)}, u32[]{:S(2)}) copy-start(s32[64]{0:T(128)} %param.29) | copy-start | bytes 772
  1.0 15.2 %copy-start.3 = (bf16[2048,128]{1,0:T(8,128)(2,1)S(1)}, bf16[2048,128]{1,0:T(8,128)(2,1)}, u32[]{:S(2)}) copy-start(bf16[2048,128]{1,0:T(8,128)(2,1)} %param.21) | copy-start | bytes 1572868
  23.2 107.1 %copy-start.4 = (bf16[512,512]{1,0:T(8,128)(2,1)S(1)}, bf16[512,512]{1,0:T(8,128)(2,1)}, u32[]{:S(2)}) copy-start(bf16[512,512]{1,0:T(8,128)(2,1)} %param.20) | copy-start | bytes 1572868
  23.2 107.1 %copy-start.5 = (bf16[512,512]{1,0:T(8,128)(2,1)S(1)}, bf16[512,512]{1,0:T(8,128)(2,1)}, u32[]{:S(2)}) copy-start(bf16[512,512]{1,0:T(8,128)(2,1)} %param.24) | copy-start | bytes 1572868
  23.2 107.6 %all-to-all-start = ((bf16[16,16,64,128]{3,2,1,0:T(8,128)(2,1)}), bf16[16,16,64,128]{3,2,1,0:T(8,128)(2,1)}, u32[]{:S(2)}, u32[]{:S(2)}) async-start(bf16[16,16,64,128]{3,2,1,0:T(8,128)(2,1)} %select_select_fusion), calls=%async_computation | async-start | bytes 8388608 | tf_op jit(solution)/shard_map/all_to_all | solution.py:69
  130.8 7.5 %copy-start.8 = (bf16[128,512]{1,0:T(8,128)(2,1)S(1)}, bf16[128,512]{1,0:T(8,128)(2,1)}, u32[]{:S(2)}) copy-start(bf16[128,512]{1,0:T(8,128)(2,1)} %param.22) | copy-start | bytes 393220
  130.8 7.5 %copy-start.9 = (f32[512]{0:T(512)S(1)}, f32[512]{0:T(512)}, u32[]{:S(2)}) copy-start(f32[512]{0:T(512)} %param.23) | copy-start | bytes 6148
  144.9 3.2 copy-start.11
  148.1 4.7 %copy-start.7 = (bf16[512,512]{1,0:T(8,128)(2,1)S(1)}, bf16[512,512]{1,0:T(8,128)(2,1)}, u32[]{:S(2)}) copy-start(bf16[512,512]{1,0:T(8,128)(2,1)} %param.25) | copy-start | bytes 1572868
  317.5 30.0 %copy-start.10 = (s32[64]{0:T(128)S(1)}, s32[64]{0:T(128)}, u32[]{:S(2)}) copy-start(s32[64]{0:T(128)} %param.31) | copy-start | bytes 772
  317.5 45.8 %copy-start.1 = (bf16[512,512]{1,0:T(8,128)(2,1)S(1)}, bf16[512,512]{1,0:T(8,128)(2,1)}, u32[]{:S(2)}) copy-start(bf16[512,512]{1,0:T(8,128)(2,1)} %param.26) | copy-start | bytes 1572868
  328.9 32.8 %all-to-all-start.1 = ((bf16[16,4,1,8,512]{4,3,1,2,0:T(8,128)(2,1)}), bf16[16,4,1,8,512]{4,3,1,2,0:T(8,128)(2,1)S(1)}, u32[]{:S(2)}, u32[]{:S(2)}) async-start(bf16[16,4,1,8,512]{4,3,1,2,0:T(8,128)(2,1)} %fusion.76), calls=%async_computation.1 | async-start | bytes 1048576 | tf_op jit(solution)/shard_map/all_to_all | solution.py:132
